TPU v7x, 32 devices: a whole 2x2x4 slice. The times are simulated.
32 devices in a mesh: parts: 2 (over x), seq: 16 (over z, y, core).
Axes of the slice: x: 2, y: 2, z: 4, core: 2. Of those that a mesh axis runs over, the one named last changes fastest.
Arguments:
- tokens: bfloat16 [131072, 512], P(('parts', 'seq')), parts along dimension 0, may hold values from -6 to 6
- w_value: bfloat16 [512, 512], replicated, may hold values from -0.25 to 0.25
- w_gate: bfloat16 [512, 512], replicated, may hold values from -0.25 to 0.25
- first_block: bfloat16 [256, 256], replicated, may hold values from -0.375 to 0.375
- second_block: bfloat16 [256, 256], replicated, may hold values from -0.375 to 0.375
- third_block: bfloat16 [256, 256], replicated, may hold values from -0.375 to 0.375
- fourth_block: bfloat16 [256, 256], replicated, may hold values from -0.375 to 0.375
- kernel: bfloat16 [512, 256, 256], P('seq'), may hold values from -6 to 6
- skip_gain: float32 [512], replicated, may hold values from 0.25 to 2
- cotangent: bfloat16 [131072, 512], P(('parts', 'seq')), parts along dimension 0, may hold values from -6 to 6
Outputs:
- grad_tokens: bfloat16 [131072, 512], P(('parts', 'seq')), parts along dimension 0
- grad_kernel: bfloat16 [1024, 256, 256], P(('parts', 'seq')), parts along dimension 0
- grad_weights: float32 [4, 512, 512], P('parts'), parts along dimension 0
- grad_skip: float32 [1024], P('parts'), parts along dimension 0
There are 2 independent parts, one for each index of `parts`. A program takes and returns all parts, laid end to end along the dimension named above; an argument that names none is the same for every part. Nothing has to cross between parts.
All inputs are finite; a program needn't handle non-finite values.
Results may differ from a plain program's by a relative error of at most 0.025.
Values may be sent and summed in bfloat16 or wider, within the bound.
A program may use at most 128 MiB of HBM per device.

v0:
```python
import jax
import jax.numpy as jnp
from jax import lax
from jax.sharding import PartitionSpec as P

D = 512
N1 = 256
N2 = 256


def on_device(
    tokens,
    w_value,
    w_gate,
    first_block,
    second_block,
    third_block,
    fourth_block,
    kernel,
    skip_gain,
    cotangent,
):
    f32 = jnp.float32
    bf16 = jnp.bfloat16
    n_devices = lax.axis_size("seq")
    rows_here = N1 // n_devices
    local_rows = tokens.shape[0]
    value = jnp.dot(tokens, w_value, preferred_element_type=f32).astype(bf16)
    gate = jnp.dot(tokens, w_gate, preferred_element_type=f32).astype(bf16)
    cube = value.reshape(rows_here, N2, D)
    section_one = jnp.einsum("abc,pb->cap", cube, first_block, preferred_element_type=f32).astype(
        bf16
    )
    spectrum = jnp.einsum(
        "cap,qa->cqp",
        lax.all_to_all(section_one, "seq", split_axis=0, concat_axis=1, tiled=True),
        second_block,
        preferred_element_type=f32,
    )
    filtered = (spectrum * kernel.astype(f32)).astype(bf16)
    section_three = jnp.einsum(
        "cqp,rq->crp", filtered, third_block, preferred_element_type=f32
    ).astype(bf16)
    split_three = section_three.reshape(section_three.shape[0], n_devices, rows_here, N2)
    conv = jnp.einsum(
        "crp,sp->rsc",
        lax.all_to_all(split_three, "seq", split_axis=1, concat_axis=0, tiled=True)[:, 0],
        fourth_block,
        preferred_element_type=f32,
    )
    mixed = conv.reshape(local_rows, D) + skip_gain * value.astype(f32)
    upstream = cotangent.astype(f32)
    d_mix = (upstream * gate.astype(f32)).astype(bf16)
    d_gate = (upstream * mixed).astype(bf16)
    d_mix_cube = d_mix.reshape(rows_here, N2, D)
    d_three = jnp.einsum(
        "rsc,sp->crp", d_mix_cube, fourth_block, preferred_element_type=f32
    ).astype(bf16)
    d_freq = jnp.einsum(
        "crp,rq->cqp",
        lax.all_to_all(d_three, "seq", split_axis=0, concat_axis=1, tiled=True),
        third_block,
        preferred_element_type=f32,
    )
    grad_kernel = (d_freq * spectrum).astype(bf16)
    d_spec = (d_freq * kernel.astype(f32)).astype(bf16)
    d_one = jnp.einsum("cqp,qa->cap", d_spec, second_block, preferred_element_type=f32).astype(bf16)
    split_one = d_one.reshape(d_one.shape[0], n_devices, rows_here, N2)
    d_cube = jnp.einsum(
        "cap,pb->abc",
        lax.all_to_all(split_one, "seq", split_axis=1, concat_axis=0, tiled=True)[:, 0],
        first_block,
        preferred_element_type=f32,
    )
    d_value = (d_cube.reshape(local_rows, D) + skip_gain * d_mix.astype(f32)).astype(bf16)
    grad_tokens = (
        jnp.dot(d_value, w_value.T, preferred_element_type=f32)
        + jnp.dot(d_gate, w_gate.T, preferred_element_type=f32)
    ).astype(bf16)
    factor = 1.0 / jnp.sqrt(jnp.asarray(N1 * N2, f32))
    value_term = jnp.dot(tokens.T, d_value, preferred_element_type=f32) * factor
    gate_term = jnp.dot(tokens.T, d_gate, preferred_element_type=f32) * factor
    skip_term = jnp.sum(d_mix.astype(f32) * value.astype(f32), axis=0) * factor
    value_total, gate_total, skip_total = (
        lax.psum(value_term.astype(jnp.bfloat16), "seq").astype(jnp.float32),
        lax.psum(gate_term.astype(jnp.bfloat16), "seq").astype(jnp.float32),
        lax.psum(skip_term.astype(jnp.bfloat16), "seq").astype(jnp.float32),
    )
    return (grad_tokens, grad_kernel, jnp.stack([value_total, gate_total]), skip_total)


def solution(mesh):
    in_specs = (
        P(("parts", "seq"), None),
        P(),
        P(),
        P(),
        P(),
        P(),
        P(),
        P("seq", None, None),
        P(),
        P(("parts", "seq"), None),
    )
    out_specs = (
        P(("parts", "seq"), None),
        P(("parts", "seq"), None, None),
        P("parts", None, None),
        P("parts"),
    )
    return jax.shard_map(
        on_device, mesh=mesh, in_specs=in_specs, out_specs=out_specs, check_vma=False
    )
```

profile of v0, /device:TPU:0, one launch (start us, length us, event | category | flops | bytes accessed | tf_op | source)
XLA Modules:
  0.0 597.8 jit_solution(15915618487453710336)
XLA Ops:
  7.2 6.0 %fusion = bf16[4096,512]{1,0:T(8,128)(2,1)S(1)} fusion(bf16[4096,512]{1,0:T(8,128)(2,1)} %param.19, bf16[4096,512]{1,0:T(8,128)(2,1)} %param.10, bf16[512,512]{1,0:T(8,128)(2,1)} %param.12), kind=kOutput, calls=%fused_computation.7 | convolution fusion | flops 2157969408 | bytes 13107200 | tf_op jit(solution)/shard_map/dot_general | solution.py:29
  16.5 4.4 copy.60
  20.9 7.5 %all-to-all-start = ((bf16[512,16,256]{2,1,0:T(8,128)(2,1)}), bf16[512,16,256]{2,1,0:T(8,128)(2,1)}, u32[]{:S(2)}, u32[]{:S(2)}) async-start(bf16[512,16,256]{2,1,0:T(8,128)(2,1)} %copy.60), calls=%async_computation | async-start | bytes 8388608 | tf_op jit(solution)/shard_map/all_to_all | solution.py:61
  28.4 4.6 convolution_convert_fusion
  36.3 4.4 copy.70
  40.7 65.3 %all-to-all-done = bf16[512,16,256]{2,1,0:T(8,128)(2,1)} async-done(((bf16[512,16,256]{2,1,0:T(8,128)(2,1)}), bf16[512,16,256]{2,1,0:T(8,128)(2,1)}, u32[]{:S(2)}, u32[]{:S(2)}) %all-to-all-start) | async-done | bytes 4194336 | tf_op jit(solution)/shard_map/all_to_all | solution.py:61
  106.0 19.7 %all-to-all-start.2 = ((bf16[512,16,256]{2,1,0:T(8,128)(2,1)}), bf16[512,16,256]{2,1,0:T(8,128)(2,1)}, u32[]{:S(2)}, u32[]{:S(2)}) async-start(bf16[512,16,256]{2,1,0:T(8,128)(2,1)} %copy.70), calls=%async_computation.2 | async-start | bytes 8388608 | tf_op jit(solution)/shard_map/all_to_all | solution.py:36
  125.7 6.4 %copy.63 = bf16[32,256,256]{1,2,0:T(8,128)(2,1)} copy(bf16[32,256,256]{2,1,0:T(8,128)(2,1)} %param.17) | data formatting | bytes 8388608 | tf_op args[7]
  132.1 4.7 copy.61
  136.8 66.4 %all-to-all-done.2 = bf16[512,16,256]{2,1,0:T(8,128)(2,1)} async-done(((bf16[512,16,256]{2,1,0:T(8,128)(2,1)}), bf16[512,16,256]{2,1,0:T(8,128)(2,1)}, u32[]{:S(2)}, u32[]{:S(2)}) %all-to-all-start.2) | async-done | bytes 4194336 | tf_op jit(solution)/shard_map/all_to_all | solution.py:36
  217.3 19.7 %all-to-all-start.3 = ((bf16[32,16,16,256]{3,2,0,1:T(8,128)(2,1)}), bf16[32,16,16,256]{3,2,0,1:T(8,128)(2,1)}, u32[]{:S(2)}, u32[]{:S(2)}) async-start(bf16[32,16,16,256]{3,2,0,1:T(8,128)(2,1)} %copy.74), calls=%async_computation.3 | async-start | bytes 8388608 | tf_op jit(solution)/shard_map/all_to_all | solution.py:47
  237.0 6.0 fusion.13
  245.4 69.2 %all-to-all-done.3 = bf16[32,16,16,256]{3,2,0,1:T(8,128)(2,1)} async-done(((bf16[32,16,16,256]{3,2,0,1:T(8,128)(2,1)}), bf16[32,16,16,256]{3,2,0,1:T(8,128)(2,1)}, u32[]{:S(2)}, u32[]{:S(2)}) %all-to-all-start.3) | async-done | bytes 4194336 | tf_op jit(solution)/shard_map/all_to_all | solution.py:47
  314.6 19.7 %all-to-all-start.1 = ((bf16[32,16,16,256]{3,2,0,1:T(8,128)(2,1)}), bf16[32,16,16,256]{3,2,0,1:T(8,128)(2,1)}, u32[]{:S(2)}, u32[]{:S(2)}) async-start(bf16[32,16,16,256]{3,2,0,1:T(8,128)(2,1)} %copy.66), calls=%async_computation.1 | async-start | bytes 8388608 | tf_op jit(solution)/shard_map/all_to_all | solution.py:71
  334.3 6.4 %copy.76 = bf16[32,256,256]{2,1,0:T(8,128)(2,1)} copy(bf16[32,256,256]{1,2,0:T(8,128)(2,1)} %get-tuple-element.25) | data formatting | bytes 8388608
  344.4 4.5 fusion.32
  348.9 62.9 %all-to-all-done.1 = bf16[32,16,16,256]{3,2,0,1:T(8,128)(2,1)} async-done(((bf16[32,16,16,256]{3,2,0,1:T(8,128)(2,1)}), bf16[32,16,16,256]{3,2,0,1:T(8,128)(2,1)}, u32[]{:S(2)}, u32[]{:S(2)}) %all-to-all-start.1) | async-done | bytes 4194336 | tf_op jit(solution)/shard_map/all_to_all | solution.py:71
  415.7 4.5 fusion.24
  420.2 10.9 %fusion.7 = (f32[512]{0:T(512)S(1)}, bf16[4096,512]{1,0:T(8,128)(2,1)}, bf16[4096,512]{1,0:T(8,128)(2,1)S(1)}) fusion(bf16[4096,512]{1,0:T(8,128)(2,1)} %copy-done.6, bf16[4096,512]{1,0:T(8,128)(2,1)} %copy-done.5, f32[512]{0:T(512)S(1)} %copy-done.13, f32[512,16,256]{0,2,1:T(8,128)} %fusion.24, f32[512,16,256]{0,2,1:T(8,128)S(1)} %bitcast.101, ...), kind=kLoop, calls=%fused_computation.14 | loop fusion | flops 25165312 | bytes 37752832 | tf_op jit(solution)/shard_map/reduce_sum | solution.py:83
  431.0 8.2 %fusion.22 = bf16[1,512,512]{1,2,0:T(8,128)(2,1)} fusion(bf16[4096,512]{1,0:T(8,128)(2,1)} %get-tuple-element.23, bf16[4096,512]{1,0:T(8,128)(2,1)} %param.10), kind=kOutput, calls=%fused_computation.31 | convolution fusion | flops 2148007936 | bytes 8912896 | tf_op jit(solution)/shard_map/dot_general | solution.py:81
  439.2 5.9 fusion.35
  448.3 47.8 %psum.23 = bf16[512]{0:T(512)(128)(2,1)S(1)} all-reduce(bf16[512]{0:T(512)(128)(2,1)S(1)} %multiply_convert_fusion), channel_id=1, replica_groups=mesh['parts'=2,'seq'=16] {'seq'}, use_global_device_ids=true, to_apply=%region_3.0 | all-reduce | flops 512 | bytes 2048 | tf_op jit(solution)/shard_map/psum | solution.py:87
  496.6 9.2 %add_convert_fusion = bf16[4096,512]{1,0:T(8,128)(2,1)} fusion(f32[4096,512]{1,0:T(8,128)} %fusion.35, bf16[4096,512]{1,0:T(8,128)(2,1)} %copy-done.3, bf16[512,512]{1,0:T(8,128)(2,1)S(1)} %copy-done.12), kind=kOutput, calls=%fused_computation.17 | convolution fusion | flops 2151677952 | bytes 17301504 | tf_op jit(solution)/shard_map/dot_general | solution.py:78
  505.8 82.0 %all-reduce.3.cloned.1.call-done = (bf16[1,512,512]{1,2,0:T(8,128)(2,1)}, bf16[1,512,512]{1,2,0:T(8,128)(2,1)}) async-done(((bf16[1,512,512]{1,2,0:T(8,128)(2,1)}, bf16[1,512,512]{1,2,0:T(8,128)(2,1)}), (bf16[1,512,512]{1,2,0:T(8,128)(2,1)}, bf16[1,512,512]{1,2,0:T(8,128)(2,1)})) %all-reduce.3.cloned.1.call-update) | async-done | bytes 1048592 | tf_op jit(solution)/shard_map/psum | solution.py:86
  (52 shorter events, 37.5 us)
Async XLA Ops:
  7.2 21.3 %copy-start = (bf16[512,512]{1,0:T(8,128)(2,1)S(1)}, bf16[512,512]{1,0:T(8,128)(2,1)}, u32[]{:S(2)}) copy-start(bf16[512,512]{1,0:T(8,128)(2,1)} %param.11) | copy-start | bytes 1572868
  7.2 8.0 %copy-start.10 = (bf16[256,256]{1,0:T(8,128)(2,1)S(1)}, bf16[256,256]{1,0:T(8,128)(2,1)}, u32[]{:S(2)}) copy-start(bf16[256,256]{1,0:T(8,128)(2,1)} %param.16) | copy-start | bytes 393220
  13.2 1.9 copy-start.5
  20.9 85.0 %all-to-all-start = ((bf16[512,16,256]{2,1,0:T(8,128)(2,1)}), bf16[512,16,256]{2,1,0:T(8,128)(2,1)}, u32[]{:S(2)}, u32[]{:S(2)}) async-start(bf16[512,16,256]{2,1,0:T(8,128)(2,1)} %copy.60), calls=%async_computation | async-start | bytes 8388608 | tf_op jit(solution)/shard_map/all_to_all | solution.py:61
  28.4 6.6 %copy-start.11 = (bf16[256,256]{1,0:T(8,128)(2,1)S(1)}, bf16[256,256]{1,0:T(8,128)(2,1)}, u32[]{:S(2)}) copy-start(bf16[256,256]{1,0:T(8,128)(2,1)} %param.13) | copy-start | bytes 393220
  33.0 2.0 copy-start.6
  106.0 97.2 %all-to-all-start.2 = ((bf16[512,16,256]{2,1,0:T(8,128)(2,1)}), bf16[512,16,256]{2,1,0:T(8,128)(2,1)}, u32[]{:S(2)}, u32[]{:S(2)}) async-start(bf16[512,16,256]{2,1,0:T(8,128)(2,1)} %copy.70), calls=%async_computation.2 | async-start | bytes 8388608 | tf_op jit(solution)/shard_map/all_to_all | solution.py:36
  203.2 3.4 copy-start.7
  203.2 3.5 copy-start.8
  206.6 1.3 copy-start.9
  208.0 5.6 copy-start.1
  208.0 5.6 copy-start.2
  217.3 97.3 %all-to-all-start.3 = ((bf16[32,16,16,256]{3,2,0,1:T(8,128)(2,1)}), bf16[32,16,16,256]{3,2,0,1:T(8,128)(2,1)}, u32[]{:S(2)}, u32[]{:S(2)}) async-start(bf16[32,16,16,256]{3,2,0,1:T(8,128)(2,1)} %copy.74), calls=%async_computation.3 | async-start | bytes 8388608 | tf_op jit(solution)/shard_map/all_to_all | solution.py:47
  314.6 97.2 %all-to-all-start.1 = ((bf16[32,16,16,256]{3,2,0,1:T(8,128)(2,1)}), bf16[32,16,16,256]{3,2,0,1:T(8,128)(2,1)}, u32[]{:S(2)}, u32[]{:S(2)}) async-start(bf16[32,16,16,256]{3,2,0,1:T(8,128)(2,1)} %copy.66), calls=%async_computation.1 | async-start | bytes 8388608 | tf_op jit(solution)/shard_map/all_to_all | solution.py:71
  334.3 253.5 %all-reduce.3.cloned.1.call-start = ((), (), s32[]{:S(2)}) async-start(), calls=%async_computation.4 | async-start | bytes 2097152 | tf_op jit(solution)/shard_map/psum | solution.py:86
  411.8 8.3 %slice-start = ((s8[8388608]{0:T(1024)(128)(4,1)}), s8[4194304]{0:T(1024)(128)(4,1)S(1)}, s32[]{:S(2)}) async-start(s8[8388608]{0:T(1024)(128)(4,1)} %bitcast.100), calls=%async_computation.5 | async-start | bytes 8388608
  415.6 4.5 slice-start.1
  415.6 4.5 copy-start.13
  431.0 14.1 %copy-start.3 = (bf16[4096,512]{1,0:T(8,128)(2,1)}, bf16[4096,512]{1,0:T(8,128)(2,1)S(1)}, u32[]{:S(2)}) copy-start(bf16[4096,512]{1,0:T(8,128)(2,1)S(1)} %get-tuple-element.24) | copy-start | bytes 12582916
  431.0 8.2 %copy-start.4 = (bf16[4096,512]{1,0:T(8,128)(2,1)S(1)}, bf16[4096,512]{1,0:T(8,128)(2,1)}, u32[]{:S(2)}) copy-start(bf16[4096,512]{1,0:T(8,128)(2,1)} %get-tuple-element.23) | copy-start | bytes 12582916
  439.2 5.9 copy-start.14
  445.1 51.5 %copy-start.12 = (bf16[512,512]{1,0:T(8,128)(2,1)S(1)}, bf16[512,512]{1,0:T(8,128)(2,1)}, u32[]{:S(2)}) copy-start(bf16[512,512]{1,0:T(8,128)(2,1)} %param.12) | copy-start | bytes 1572868
Sparse Core Ops, SparseCore 0:
  496.8 90.9 all-reduce.2
where the time goes:
time: 599 us; the launch traced here: 598 us
  waiting for transfers between devices  346 us (58%)
  starting transfers between devices  66.6 us (11%)
  matrix products  60.6 us (10%)
  local copies, waits for them, and re-layouts  50.1 us (8%)
  blocking collectives  47.8 us (8%)
  between operations  14.3 us (2%)
  other arithmetic  12.8 us (2%)
    psum x1, waiting for transfers between devices, on_device(): lax.psum(gate_term.astype(jnp.bfloat16), 'seq').astype(jnp.float32)  82 us
    all_to_all x1, waiting for transfers between devices, on_device(): lax.all_to_all(split_three, 'seq', split_axis=1, concat_axis=0, tiled=True)  69.2 us
    all_to_all x1, waiting for transfers between devices, on_device(): lax.all_to_all(section_one, 'seq', split_axis=0, concat_axis=1, tiled=True)  66.4 us
    all_to_all x1, waiting for transfers between devices, on_device(): lax.all_to_all(d_three, 'seq', split_axis=0, concat_axis=1, tiled=True)  65.3 us
    all_to_all x1, waiting for transfers between devices, on_device(): lax.all_to_all(split_one, 'seq', split_axis=1, concat_axis=0, tiled=True)  62.9 us
    psum x1, blocking collectives, on_device(): lax.psum(skip_term.astype(jnp.bfloat16), 'seq').astype(jnp.float32)  47.8 us
    unnamed x37, local copies, waits for them, and re-layouts  21.5 us
    all_to_all x1, starting transfers between devices, on_device(): lax.all_to_all(split_three, 'seq', split_axis=1, concat_axis=0, tiled=True)  19.7 us
  transfers between devices with their start and end apart: 5, of which 5 were waited for; matrix products, arithmetic and copies ran while one was open for 9% of the time, Pallas kernels for 0%

commit v1 on v0

--- a/solution.py
+++ b/solution.py
@@ -6,6 +6,12 @@
 D = 512
 N1 = 256
 N2 = 256
+
+
+def gather_and_add(shard, axis):
+    parts = lax.all_gather(shard, axis, axis=0, tiled=False)
+    acc = parts.sum(axis=0)
+    return acc
 
 
 def on_device(
@@ -83,7 +89,7 @@
     skip_term = jnp.sum(d_mix.astype(f32) * value.astype(f32), axis=0) * factor
     value_total, gate_total, skip_total = (
         lax.psum(value_term.astype(jnp.bfloat16), "seq").astype(jnp.float32),
-        lax.psum(gate_term.astype(jnp.bfloat16), "seq").astype(jnp.float32),
+        gather_and_add(gate_term.astype(jnp.bfloat16), "seq").astype(jnp.float32),
         lax.psum(skip_term.astype(jnp.bfloat16), "seq").astype(jnp.float32),
     )
     return (grad_tokens, grad_kernel, jnp.stack([value_total, gate_total]), skip_total)

time: 599 us -> 640 us (1.068)
  waiting for transfers between devices: 346 us -> 360 us
  local copies, waits for them, and re-layouts: 50.1 us -> 63.2 us
  other arithmetic: 12.8 us -> 21 us
    all_gather x0 -> x1, waiting for transfers between devices: none -> 16.5 us  [gather_and_add(): parts = lax.all_gather(shard, axis, axis=0, tiled=False)]
    unnamed x37 -> x38, local copies, waits for them, and re-layouts: 21.5 us -> 34.6 us
    psum x1, waiting for transfers between devices: 82 us -> 73 us  [on_device(): lax.psum(value_term.astype(jnp.bfloat16), 'seq').astype(jnp.float32)]
    reduce_sum x0 -> x1, other arithmetic: none -> 8.35 us  [gather_and_add(): acc = parts.sum(axis=0)]
    all_to_all x1, waiting for transfers between devices: 62.9 us -> 69.3 us  [on_device(): lax.all_to_all(split_one, 'seq', split_axis=1, concat_axis=0, tiled=True)]
  transfers between devices with their start and end apart: 5 -> 6, of which waited for: 5 -> 6; matrix products, arithmetic and copies ran while one was open for 9% -> 13% of each run, Pallas kernels for 0% -> 0%
where the time goes in v1:
time: 640 us; the launch traced here: 635 us
  waiting for transfers between devices  360 us (56%)
  starting transfers between devices  67.3 us (11%)
  local copies, waits for them, and re-layouts  63.2 us (10%)
  matrix products  59.6 us (9%)
  blocking collectives  49.3 us (8%)
  other arithmetic  21 us (3%)
  between operations  14.5 us (2%)
    psum x1, waiting for transfers between devices, on_device(): lax.psum(value_term.astype(jnp.bfloat16), 'seq').astype(jnp.float32)  73 us
    all_to_all x1, waiting for transfers between devices, on_device(): lax.all_to_all(split_one, 'seq', split_axis=1, concat_axis=0, tiled=True)  69.3 us
    all_to_all x1, waiting for transfers between devices, on_device(): lax.all_to_all(split_three, 'seq', split_axis=1, concat_axis=0, tiled=True)  69.2 us
    all_to_all x1, waiting for transfers between devices, on_device(): lax.all_to_all(section_one, 'seq', split_axis=0, concat_axis=1, tiled=True)  66.4 us
    all_to_all x1, waiting for transfers between devices, on_device(): lax.all_to_all(d_three, 'seq', split_axis=0, concat_axis=1, tiled=True)  65.2 us
    psum x1, blocking collectives, on_device(): lax.psum(skip_term.astype(jnp.bfloat16), 'seq').astype(jnp.float32)  49.3 us
    unnamed x38, local copies, waits for them, and re-layouts  34.6 us
    all_to_all x1, starting transfers between devices, on_device(): lax.all_to_all(split_three, 'seq', split_axis=1, concat_axis=0, tiled=True)  19.9 us
  transfers between devices with their start and end apart: 6, of which 6 were waited for; matrix products, arithmetic and copies ran while one was open for 13% of the time, Pallas kernels for 0%

profile of v1, /device:TPU:0, one launch (start us, length us, event | category | flops | bytes accessed | tf_op | source)
XLA Modules:
  0.0 634.6 jit_solution(11578867936475679422)
XLA Ops:
  7.2 6.0 fusion
  21.0 8.0 %all-to-all-start = ((bf16[512,16,256]{2,1,0:T(8,128)(2,1)}), bf16[512,16,256]{2,1,0:T(8,128)(2,1)}, u32[]{:S(2)}, u32[]{:S(2)}) async-start(bf16[512,16,256]{2,1,0:T(8,128)(2,1)} %copy.60), calls=%async_computation | async-start | bytes 8388608 | tf_op jit(solution)/shard_map/all_to_all | solution.py:67
  29.0 4.6 convolution_convert_fusion
  41.3 65.2 %all-to-all-done = bf16[512,16,256]{2,1,0:T(8,128)(2,1)} async-done(((bf16[512,16,256]{2,1,0:T(8,128)(2,1)}), bf16[512,16,256]{2,1,0:T(8,128)(2,1)}, u32[]{:S(2)}, u32[]{:S(2)}) %all-to-all-start) | async-done | bytes 4194336 | tf_op jit(solution)/shard_map/all_to_all | solution.py:67
  106.5 19.7 %all-to-all-start.2 = ((bf16[512,16,256]{2,1,0:T(8,128)(2,1)}), bf16[512,16,256]{2,1,0:T(8,128)(2,1)}, u32[]{:S(2)}, u32[]{:S(2)}) async-start(bf16[512,16,256]{2,1,0:T(8,128)(2,1)} %copy.70), calls=%async_computation.2 | async-start | bytes 8388608 | tf_op jit(solution)/shard_map/all_to_all | solution.py:42
  126.2 6.4 %copy.63 = bf16[32,256,256]{1,2,0:T(8,128)(2,1)} copy(bf16[32,256,256]{2,1,0:T(8,128)(2,1)} %param.17) | data formatting | bytes 8388608 | tf_op args[7]
  132.6 4.7 copy.61
  137.3 66.4 %all-to-all-done.2 = bf16[512,16,256]{2,1,0:T(8,128)(2,1)} async-done(((bf16[512,16,256]{2,1,0:T(8,128)(2,1)}), bf16[512,16,256]{2,1,0:T(8,128)(2,1)}, u32[]{:S(2)}, u32[]{:S(2)}) %all-to-all-start.2) | async-done | bytes 4194336 | tf_op jit(solution)/shard_map/all_to_all | solution.py:42
  217.9 19.9 %all-to-all-start.3 = ((bf16[32,16,16,256]{3,2,0,1:T(8,128)(2,1)}), bf16[32,16,16,256]{3,2,0,1:T(8,128)(2,1)}, u32[]{:S(2)}, u32[]{:S(2)}) async-start(bf16[32,16,16,256]{3,2,0,1:T(8,128)(2,1)} %copy.74), calls=%async_computation.3 | async-start | bytes 8388608 | tf_op jit(solution)/shard_map/all_to_all | solution.py:53
  237.7 6.0 fusion.13
  246.1 69.2 %all-to-all-done.3 = bf16[32,16,16,256]{3,2,0,1:T(8,128)(2,1)} async-done(((bf16[32,16,16,256]{3,2,0,1:T(8,128)(2,1)}), bf16[32,16,16,256]{3,2,0,1:T(8,128)(2,1)}, u32[]{:S(2)}, u32[]{:S(2)}) %all-to-all-start.3) | async-done | bytes 4194336 | tf_op jit(solution)/shard_map/all_to_all | solution.py:53
  315.3 19.7 %all-to-all-start.1 = ((bf16[32,16,16,256]{3,2,0,1:T(8,128)(2,1)}), bf16[32,16,16,256]{3,2,0,1:T(8,128)(2,1)}, u32[]{:S(2)}, u32[]{:S(2)}) async-start(bf16[32,16,16,256]{3,2,0,1:T(8,128)(2,1)} %copy.66), calls=%async_computation.1 | async-start | bytes 8388608 | tf_op jit(solution)/shard_map/all_to_all | solution.py:77
  338.7 4.5 fusion.32
  343.2 69.3 %all-to-all-done.1 = bf16[32,16,16,256]{3,2,0,1:T(8,128)(2,1)} async-done(((bf16[32,16,16,256]{3,2,0,1:T(8,128)(2,1)}), bf16[32,16,16,256]{3,2,0,1:T(8,128)(2,1)}, u32[]{:S(2)}, u32[]{:S(2)}) %all-to-all-start.1) | async-done | bytes 4194336 | tf_op jit(solution)/shard_map/all_to_all | solution.py:77
  420.9 10.9 %fusion.7 = (f32[512]{0:T(512)S(1)}, bf16[4096,512]{1,0:T(8,128)(2,1)}, bf16[4096,512]{1,0:T(8,128)(2,1)S(1)}) fusion(bf16[4096,512]{1,0:T(8,128)(2,1)} %copy-done.6, bf16[4096,512]{1,0:T(8,128)(2,1)} %copy-done.5, f32[512]{0:T(512)S(1)} %copy-done.13, f32[512,16,256]{0,2,1:T(8,128)} %fusion.24, f32[512,16,256]{0,2,1:T(8,128)S(1)} %bitcast.105, ...), kind=kLoop, calls=%fused_computation.14 | loop fusion | flops 25165312 | bytes 37752832 | tf_op jit(solution)/shard_map/reduce_sum | solution.py:89
  433.7 5.3 fusion.21
  439.2 6.4 %copy.76 = bf16[32,256,256]{2,1,0:T(8,128)(2,1)} copy(bf16[32,256,256]{1,2,0:T(8,128)(2,1)} %get-tuple-element.23) | data formatting | bytes 8388608
  445.6 49.3 %psum.15 = bf16[512]{0:T(512)(128)(2,1)S(1)} all-reduce(bf16[512]{0:T(512)(128)(2,1)S(1)} %multiply_convert_fusion), channel_id=1, replica_groups=mesh['parts'=2,'seq'=16] {'seq'}, use_global_device_ids=true, to_apply=%region_3.0 | all-reduce | flops 512 | bytes 2048 | tf_op jit(solution)/shard_map/psum | solution.py:93
  495.5 7.9 %fusion.35 = f32[4096,512]{1,0:T(8,128)} fusion(bf16[4096,512]{1,0:T(8,128)(2,1)} %get-tuple-element.21, bf16[512,512]{1,0:T(8,128)(2,1)S(1)} %copy-done), kind=kOutput, calls=%fused_computation.47 | convolution fusion | flops 2147483648 | bytes 13107200 | tf_op jit(solution)/shard_map/dot_general | solution.py:83
  506.6 9.1 %add_convert_fusion = bf16[4096,512]{1,0:T(8,128)(2,1)} fusion(f32[4096,512]{1,0:T(8,128)} %fusion.35, bf16[4096,512]{1,0:T(8,128)(2,1)} %copy-done.3, bf16[512,512]{1,0:T(8,128)(2,1)S(1)} %copy-done.12), kind=kOutput, calls=%fused_computation.18 | convolution fusion | flops 2151677952 | bytes 17301504 | tf_op jit(solution)/shard_map/dot_general | solution.py:84
  515.7 16.5 %all-gather.3.cloned.1.call-done = bf16[8192,512]{0,1:T(8,128)(2,1)} async-done(((bf16[512,512]{0,1:T(8,128)(2,1)}), bf16[8192,512]{0,1:T(8,128)(2,1)}) %all-gather.3.cloned.1.call-update) | async-done | bytes 8388624 | tf_op jit(solution)/shard_map/all_gather | solution.py:12
  532.2 11.0 %copy.88 = bf16[64,8,16,512]{3,2,1,0:T(8,128)(2,1)} copy(bf16[64,8,16,512]{3,1,2,0:T(8,128)(2,1)} %bitcast.114) | data formatting | bytes 16777216
  543.2 8.4 %bitcast_reduce_fusion = bf16[512,512]{0,1:T(8,128)(2,1)S(1)} fusion(bf16[64,8,16,512]{3,2,1,0:T(8,128)(2,1)} %copy.88), kind=kLoop, calls=%fused_computation.15 | loop fusion | flops 3932160 | bytes 8912896 | tf_op jit(solution)/shard_map/reduce_sum | solution.py:13
  551.6 73.0 %all-reduce.2.cloned.1.call-done = bf16[1,512,512]{1,2,0:T(8,128)(2,1)} async-done(((bf16[1,512,512]{1,2,0:T(8,128)(2,1)}), bf16[1,512,512]{1,2,0:T(8,128)(2,1)}) %all-reduce.2.cloned.1.call-update) | async-done | bytes 524304 | tf_op jit(solution)/shard_map/psum | solution.py:91
  (57 shorter events, 52.8 us)
Async XLA Ops:
  7.2 21.8 %copy-start = (bf16[512,512]{1,0:T(8,128)(2,1)S(1)}, bf16[512,512]{1,0:T(8,128)(2,1)}, u32[]{:S(2)}) copy-start(bf16[512,512]{1,0:T(8,128)(2,1)} %param.11) | copy-start | bytes 1572868
  7.2 8.1 %copy-start.10 = (bf16[256,256]{1,0:T(8,128)(2,1)S(1)}, bf16[256,256]{1,0:T(8,128)(2,1)}, u32[]{:S(2)}) copy-start(bf16[256,256]{1,0:T(8,128)(2,1)} %param.16) | copy-start | bytes 393220
  13.2 2.0 copy-start.5
  21.0 85.5 %all-to-all-start = ((bf16[512,16,256]{2,1,0:T(8,128)(2,1)}), bf16[512,16,256]{2,1,0:T(8,128)(2,1)}, u32[]{:S(2)}, u32[]{:S(2)}) async-start(bf16[512,16,256]{2,1,0:T(8,128)(2,1)} %copy.60), calls=%async_computation | async-start | bytes 8388608 | tf_op jit(solution)/shard_map/all_to_all | solution.py:67
  29.0 6.6 %copy-start.11 = (bf16[256,256]{1,0:T(8,128)(2,1)S(1)}, bf16[256,256]{1,0:T(8,128)(2,1)}, u32[]{:S(2)}) copy-start(bf16[256,256]{1,0:T(8,128)(2,1)} %param.13) | copy-start | bytes 393220
  33.6 2.0 copy-start.6
  106.5 97.2 %all-to-all-start.2 = ((bf16[512,16,256]{2,1,0:T(8,128)(2,1)}), bf16[512,16,256]{2,1,0:T(8,128)(2,1)}, u32[]{:S(2)}, u32[]{:S(2)}) async-start(bf16[512,16,256]{2,1,0:T(8,128)(2,1)} %copy.70), calls=%async_computation.2 | async-start | bytes 8388608 | tf_op jit(solution)/shard_map/all_to_all | solution.py:42
  203.7 3.4 copy-start.7
  203.7 3.5 copy-start.8
  207.2 1.3 copy-start.9
  208.5 5.6 copy-start.1
  208.5 5.6 copy-start.2
  217.9 97.4 %all-to-all-start.3 = ((bf16[32,16,16,256]{3,2,0,1:T(8,128)(2,1)}), bf16[32,16,16,256]{3,2,0,1:T(8,128)(2,1)}, u32[]{:S(2)}, u32[]{:S(2)}) async-start(bf16[32,16,16,256]{3,2,0,1:T(8,128)(2,1)} %copy.74), calls=%async_computation.3 | async-start | bytes 8388608 | tf_op jit(solution)/shard_map/all_to_all | solution.py:53
  315.3 97.2 %all-to-all-start.1 = ((bf16[32,16,16,256]{3,2,0,1:T(8,128)(2,1)}), bf16[32,16,16,256]{3,2,0,1:T(8,128)(2,1)}, u32[]{:S(2)}, u32[]{:S(2)}) async-start(bf16[32,16,16,256]{3,2,0,1:T(8,128)(2,1)} %copy.66), calls=%async_computation.1 | async-start | bytes 8388608 | tf_op jit(solution)/shard_map/all_to_all | solution.py:77
  335.0 197.3 %all-gather.3.cloned.1.call-start = ((), (), s32[]{:S(2)}) async-start(), calls=%async_computation.5 | async-start | bytes 8912896 | tf_op jit(solution)/shard_map/all_gather | solution.py:12
  412.5 8.4 %slice-start = ((s8[8388608]{0:T(1024)(128)(4,1)}), s8[4194304]{0:T(1024)(128)(4,1)S(1)}, s32[]{:S(2)}) async-start(s8[8388608]{0:T(1024)(128)(4,1)} %bitcast.104), calls=%async_computation.6 | async-start | bytes 8388608
  416.3 4.6 slice-start.1
  416.3 4.5 copy-start.13
  431.7 2.0 copy-start.3
  439.1 185.4 %all-reduce.2.cloned.1.call-start = ((), (), s32[]{:S(2)}) async-start(), calls=%async_computation.4 | async-start | bytes 1048576 | tf_op jit(solution)/shard_map/psum | solution.py:91
  495.5 7.9 %copy-start.4 = (bf16[4096,512]{1,0:T(8,128)(2,1)S(1)}, bf16[4096,512]{1,0:T(8,128)(2,1)}, u32[]{:S(2)}) copy-start(bf16[4096,512]{1,0:T(8,128)(2,1)} %get-tuple-element.21) | copy-start | bytes 12582916
  495.5 7.9 %copy-start.14 = (bf16[4096,512]{1,0:T(8,128)(2,1)S(1)}, bf16[4096,512]{1,0:T(8,128)(2,1)}, u32[]{:S(2)}) copy-start(bf16[4096,512]{1,0:T(8,128)(2,1)} %param.10) | copy-start | bytes 12582916
  503.4 3.2 copy-start.12
Sparse Core Ops, SparseCore 0:
  439.2 92.9 all-gather.2
  535.6 88.8 all-reduce.1
